TPU v7x, 128 devices: a whole 4x4x4 slice. The times are simulated.
128 devices in a mesh: section: 8 (over y, core), fsdp: 16 (over x, z).
Axes of the slice: x: 4, y: 4, z: 4, core: 2. Of those that a mesh axis runs over, the one named last changes fastest.
Arguments:
- layer_input: bfloat16 [8, 8192, 2048], P('section', 'fsdp'), may hold values from -6 to 6
- resid_grad: bfloat16 [8, 8192, 2048], P('section', 'fsdp'), may hold values from -6 to 6
- qkv_grad: bfloat16 [8, 8192, 3072], P('section', 'fsdp'), may hold values from -6 to 6
- prev_input: bfloat16 [8, 8192, 2048], P('section', 'fsdp'), may hold values from -6 to 6
- prev_qkv_grad: bfloat16 [8, 8192, 3072], P('section', 'fsdp'), may hold values from -0.059814453 to 0.059814453
- qkv_weight: bfloat16 [8, 2048, 3072], P('section', 'fsdp'), may hold values from -0.125 to 0.125
- norm_gain: float32 [8, 2048], P('section'), may hold values from 0.1 to 1.9
Outputs:
- upstream_grad: bfloat16 [8, 8192, 2048], P('section', 'fsdp')
- weight_grad: float32 [8, 2048, 3072], P('section', 'fsdp')
- gain_grad: float32 [8, 2048], P('section')
All inputs are finite; a program needn't handle non-finite values.
Results may differ from a plain program's by a relative error of at most 0.018.
Values may be sent and summed in bfloat16 or wider, within the bound.
A program may use at most 128 MiB of HBM per device.

v0:
```python
import jax
import jax.numpy as jnp
from jax import lax
from jax.sharding import PartitionSpec as P

EPS = 1e-05


def from_behind(block, axis, distance):
    devices = range(lax.axis_size(axis))
    route = [(i - distance, i) for i in devices if i - distance in devices]
    return lax.ppermute(block, axis, route)


def row_scale(rows):
    values = rows.astype(jnp.float32)
    return lax.rsqrt(jnp.mean(values * values, axis=-1, keepdims=True) + EPS)


def transpose_product(grads, piece):
    return lax.dot_general(
        grads, piece, (((1,), (1,)), ((), ())), preferred_element_type=jnp.float32
    )


def local(layer_input, resid_grad, qkv_grad, prev_input, prev_qkv_grad, qkv_weight, norm_gain):
    rows_now = layer_input[0]
    grads_now = qkv_grad[0]
    rows_prev = prev_input[0]
    grads_prev = prev_qkv_grad[0]
    weight_rows = qkv_weight[0]
    gain = norm_gain[0]
    owned = weight_rows.shape[0]
    prev_scale = row_scale(rows_prev)
    prev_normed = (rows_prev.astype(jnp.float32) * prev_scale * gain[None, :]).astype(jnp.bfloat16)
    direction = transpose_product(
        grads_now, lax.all_gather(weight_rows, "fsdp", axis=0, tiled=True)
    )
    scale = row_scale(rows_now)
    values = rows_now.astype(jnp.float32)
    gained = gain[None, :] * direction
    inner = jnp.mean(gained * values, axis=-1, keepdims=True)
    local_grad = (
        resid_grad[0].astype(jnp.float32) + scale * gained - values * scale * scale * scale * inner
    ).astype(jnp.bfloat16)
    upstream_grad = from_behind(local_grad, "section", -1)
    weight_grad = lax.psum_scatter(
        lax.dot_general(
            prev_normed, grads_prev, (((0,), (0,)), ((), ())), preferred_element_type=jnp.float32
        ).astype(jnp.bfloat16),
        "fsdp",
        scatter_dimension=0,
        tiled=True,
    ).astype(jnp.float32)
    owned_gain = lax.dynamic_slice_in_dim(gain, lax.axis_index("fsdp") * owned, owned, 0)
    gain_part = jnp.sum(weight_rows.astype(jnp.float32) * weight_grad, axis=1) / owned_gain
    gain_grad = lax.all_gather(gain_part, "fsdp", axis=0, tiled=True)
    return (upstream_grad[None], weight_grad[None], gain_grad[None])


def solution(mesh):
    placed = (
        P("section", "fsdp", None),
        P("section", "fsdp", None),
        P("section", "fsdp", None),
        P("section", "fsdp", None),
        P("section", "fsdp", None),
        P("section", "fsdp", None),
        P("section", None),
    )
    return jax.shard_map(
        local,
        mesh=mesh,
        in_specs=placed,
        out_specs=(P("section", "fsdp", None), P("section", "fsdp", None), P("section", None)),
        check_vma=False,
    )
```

profile of v0, /device:TPU:0, one launch (start us, length us, event | category | flops | bytes accessed | tf_op | source)
XLA Modules:
  0.0 234.6 jit_solution(13687583729323604503)
XLA Ops:
  7.2 0.0 copy-start
  7.2 0.0 all-gather.4.cloned.1.call-start
  7.2 0.7 all-gather.4.cloned.1.call-update
  7.9 0.0 reduce-scatter.2.cloned.1.call-start
  8.0 2.2 fusion.2
  10.2 0.0 copy-done
  10.2 11.6 %convolution_convert_fusion = bf16[2048,3072]{1,0:T(8,128)(2,1)} fusion(bf16[1,512,3072]{2,1,0:T(8,128)(2,1)S(1)} %copy-done, bf16[1,512,2048]{2,1,0:T(8,128)(2,1)} %param.10, f32[2048]{0:T(1024)} %bitcast.39, f32[512]{0:T(512)S(1)} %add_rsqrt_fusion), kind=kOutput, calls=%fused_computation.2 | convolution fusion | flops 6452936704 | bytes 17836032 | tf_op jit(solution)/shard_map/dot_general | solution.py:48
  21.8 0.0 copy-start.3
  21.8 0.0 reduce-scatter.2.cloned.1.call-update
  21.8 81.0 %all-gather.4.cloned.1.call-done = bf16[1,2048,3072]{2,1,0:T(8,128)(2,1)} async-done(((bf16[1,128,3072]{2,1,0:T(8,128)(2,1)}), bf16[1,2048,3072]{2,1,0:T(8,128)(2,1)}) %all-gather.4.cloned.1.call-update) | async-done | bytes 12582928 | tf_op jit(solution)/shard_map/all_gather | solution.py:37
  102.8 0.0 copy-done.3
  102.8 0.0 copy-start.2
  102.9 11.3 %fusion.5 = (f32[512]{0:T(512)S(1)}, f32[512]{0:T(512)S(1)}, f32[512,2048]{1,0:T(8,128)S(1)}) fusion(bf16[1,512,2048]{2,1,0:T(8,128)(2,1)} %param.7, f32[2048]{0:T(1024)S(1)} %bitcast.40, bf16[1,2048,3072]{2,1,0:T(8,128)(2,1)} %all-gather.4.cloned.1.call-done, bf16[1,512,3072]{2,1,0:T(8,128)(2,1)} %param.9), kind=kOutput, calls=%fused_computation.11 | convolution fusion | flops 6448741376 | bytes 22032384 | tf_op jit(solution)/shard_map/dot_general | solution.py:21
  114.2 0.0 copy-done.1
  114.2 0.0 copy-done.2
  114.2 3.1 %fusion.10 = bf16[512,2048]{1,0:T(8,128)(2,1)} fusion(f32[512,2048]{1,0:T(8,128)S(1)} %get-tuple-element.5, bf16[1,512,2048]{2,1,0:T(8,128)(2,1)S(1)} %copy-done.2, bf16[1,512,2048]{2,1,0:T(8,128)(2,1)S(1)} %copy-done.1, f32[512]{0:T(512)S(1)} %get-tuple-element.7, f32[2048]{0:T(1024)S(1)} %bitcast.41, f32[512]{0:T(512)S(1)} %get-tuple-element.6), kind=kLoop, calls=%fused_computation.16 | loop fusion | flops 11534336 | bytes 10498048 | tf_op jit(solution)/shard_map/convert_element_type | solution.py:45
  117.3 1.3 collective-permute-start
  118.6 82.1 %reduce-scatter.2.cloned.1.call-done = bf16[128,3072]{1,0:T(8,128)(2,1)} async-done(((bf16[2048,3072]{1,0:T(8,128)(2,1)}), bf16[128,3072]{1,0:T(8,128)(2,1)}) %reduce-scatter.2.cloned.1.call-update) | async-done | bytes 786448 | tf_op jit(solution)/shard_map/reduce_scatter | solution.py:47
  200.6 1.7 fusion.18
  202.3 19.3 %all-gather.1 = f32[16,1,128]{2,1,0:T(1,128)S(1)} all-gather(f32[1,1,128]{2,1,0:T(1,128)S(1)} %fusion.19), channel_id=1, replica_groups=mesh['section'=8,'fsdp'=16] {'fsdp'}, dimensions={0}, use_global_device_ids=true | all-gather | bytes 8704 | tf_op jit(solution)/shard_map/all_gather | solution.py:57
  221.6 2.4 %convert_bitcast_fusion = f32[1,128,3072]{2,1,0:T(8,128)} fusion(bf16[128,3072]{1,0:T(8,128)(2,1)} %reduce-scatter.2.cloned.1.call-done), kind=kLoop, calls=%fused_computation.25 | loop fusion | flops 393216 | bytes 2359296 | tf_op jit(solution)/shard_map/broadcast_in_dim | solution.py:58
  224.0 0.0 collective-permute-done
  224.0 3.2 %copy.12 = bf16[1,512,2048]{2,1,0:T(8,128)(2,1)} copy(bf16[1,512,2048]{2,1,0:T(8,128)(2,1)} %bitcast.6) | data formatting | bytes 4194304
  227.2 0.6 copy.13
  (4 shorter events, 0.0 us)
Async XLA Ops:
  7.2 3.0 %copy-start = (bf16[1,512,3072]{2,1,0:T(8,128)(2,1)S(1)}, bf16[1,512,3072]{2,1,0:T(8,128)(2,1)}, u32[]{:S(2)}) copy-start(bf16[1,512,3072]{2,1,0:T(8,128)(2,1)} %param.11) | copy-start | bytes 9437188
  7.2 95.7 %all-gather.4.cloned.1.call-start = ((), (), s32[]{:S(2)}) async-start(), calls=%async_computation.2 | async-start | bytes 13369344 | tf_op jit(solution)/shard_map/all_gather | solution.py:37
  7.9 192.7 %reduce-scatter.2.cloned.1.call-start = ((), (), s32[]{:S(2)}) async-start(), calls=%async_computation.1 | async-start | bytes 13369344 | tf_op jit(solution)/shard_map/reduce_scatter | solution.py:47
  21.8 81.1 %copy-start.3 = (f32[1,2048]{1,0:T(1,128)S(1)}, f32[1,2048]{1,0:T(1,128)}, u32[]{:S(2)}) copy-start(f32[1,2048]{1,0:T(1,128)} %param.13) | copy-start | bytes 24580
  102.8 11.3 %copy-start.1 = (bf16[1,512,2048]{2,1,0:T(8,128)(2,1)S(1)}, bf16[1,512,2048]{2,1,0:T(8,128)(2,1)}, u32[]{:S(2)}) copy-start(bf16[1,512,2048]{2,1,0:T(8,128)(2,1)} %param.7) | copy-start | bytes 6291460
  102.8 11.3 %copy-start.2 = (bf16[1,512,2048]{2,1,0:T(8,128)(2,1)S(1)}, bf16[1,512,2048]{2,1,0:T(8,128)(2,1)}, u32[]{:S(2)}) copy-start(bf16[1,512,2048]{2,1,0:T(8,128)(2,1)} %param.8) | copy-start | bytes 6291460
  117.3 106.7 %collective-permute-start = (bf16[512,2048]{1,0:T(8,128)(2,1)}, bf16[512,2048]{1,0:T(8,128)(2,1)}, u32[]{:S(2)}, u32[]{:S(2)}) collective-permute-start(bf16[512,2048]{1,0:T(8,128)(2,1)} %fusion.10), channel_id=1, source_target_pairs={{16,0},{32,16},{48,32},{64,48},{80,64},{96,80},{112,96},{17,1},{33... | collective-permute-start | bytes 6291464 | tf_op jit(solution)/shard_map/ppermute | solution.py:12
Sparse Core Ops, SparseCore 0:
  10.2 92.5 all-gather.3
  106.3 94.3 reduce-scatter.1
where the time goes:
time: 235 us
  waiting for transfers between devices  164 us (70%)
  matrix products  22.9 us (10%)
  blocking collectives  19.3 us (8%)
  between operations  14.1 us (6%)
  other arithmetic  9.45 us (4%)
  local copies, waits for them, and re-layouts  3.78 us (2%)
    reduce_scatter x1, waiting for transfers between devices, local(): lax.psum_scatter(lax.dot_general(prev_normed, grads_prev, (((0,), (0,)),...  82.1 us
    all_gather x1, waiting for transfers between devices, local(): lax.all_gather(weight_rows, 'fsdp', axis=0, tiled=True)  81 us
    all_gather x1, blocking collectives, local(): gain_grad = lax.all_gather(gain_part, 'fsdp', axis=0, tiled=True)  19.3 us
    dot_general x1, matrix products, local(): lax.dot_general(prev_normed, grads_prev, (((0,), (0,)), ((), ())), prefer...  11.6 us
    dot_general x1, matrix products, transpose_product(): lax.dot_general(grads, piece, (((1,), (1,)), ((), ())), preferred_element...  11.3 us
  transfers between devices with their start and end apart: 3, of which 2 were waited for; matrix products, arithmetic and copies ran while one was open for 14% of the time, Pallas kernels for 0%

commit v1 on v0

--- a/solution.py
+++ b/solution.py
@@ -2,6 +2,7 @@
 import jax.numpy as jnp
 from jax import lax
 from jax.sharding import PartitionSpec as P
+from jax.lax import all_to_all, axis_size
 
 EPS = 1e-05
 
@@ -33,9 +34,13 @@
     owned = weight_rows.shape[0]
     prev_scale = row_scale(rows_prev)
     prev_normed = (rows_prev.astype(jnp.float32) * prev_scale * gain[None, :]).astype(jnp.bfloat16)
-    direction = transpose_product(
-        grads_now, lax.all_gather(weight_rows, "fsdp", axis=0, tiled=True)
-    )
+
+    def order_node_up(block_here, which_dim):
+        moved = all_to_all(jnp.stack([block_here] * axis_size("fsdp"), axis=0), "fsdp", 0, 0)
+        known = jnp.concatenate(moved, which_dim)
+        return known
+
+    direction = transpose_product(grads_now, order_node_up(weight_rows, 0))
     scale = row_scale(rows_now)
     values = rows_now.astype(jnp.float32)
     gained = gain[None, :] * direction

time: 235 us -> 288 us (1.23); the launches traced: 235 us -> 284 us
  blocking collectives: 19.3 us -> 204 us
  waiting for transfers between devices: 164 us -> 21.2 us
  local copies, waits for them, and re-layouts: 3.78 us -> 11.2 us
    all_to_all x0 -> x1, blocking collectives: none -> 184 us  [order_node_up(): all_to_all(jnp.stack([block_here] * axis_size('fsdp'), axis=0), 'fsdp', 0...]
    all_gather x1 -> x0, waiting for transfers between devices: 81 us -> none  [local(): lax.all_gather(weight_rows, 'fsdp', axis=0, tiled=True)]
    reduce_scatter x1, waiting for transfers between devices: 82.1 us -> 16.1 us  [local(): lax.psum_scatter(lax.dot_general(prev_normed, grads_prev, (((0,), (0,)),...]
    another operation x0 -> x1, local copies, waits for them, and re-layouts: none -> 7.2 us  [order_node_up(): jnp.stack([block_here] * axis_size('fsdp'), axis=0)]
    ppermute x1, waiting for transfers between devices: 0.01 us -> 5.09 us  [from_behind(): return lax.ppermute(block, axis, route)]
  transfers between devices with their start and end apart: 3 -> 2, of which waited for: 2 -> 2; matrix products, arithmetic and copies ran while one was open for 14% -> 8% of each run, Pallas kernels for 0% -> 0%
where the time goes in v1:
time: 288 us; the launch traced here: 284 us
  blocking collectives  204 us (71%)
  waiting for transfers between devices  21.2 us (7%)
  matrix products  20.6 us (7%)
  between operations  14.1 us (5%)
  other arithmetic  11.8 us (4%)
  local copies, waits for them, and re-layouts  11.2 us (4%)
    all_to_all x1, blocking collectives, order_node_up(): all_to_all(jnp.stack([block_here] * axis_size('fsdp'), axis=0), 'fsdp', 0...  184 us
    all_gather x1, blocking collectives, local(): gain_grad = lax.all_gather(gain_part, 'fsdp', axis=0, tiled=True)  19.4 us
    reduce_scatter x1, waiting for transfers between devices, local(): lax.psum_scatter(lax.dot_general(prev_normed, grads_prev, (((0,), (0,)),...  16.1 us
    dot_general x1, matrix products, local(): lax.dot_general(prev_normed, grads_prev, (((0,), (0,)), ((), ())), prefer...  11.6 us
    dot_general x1, matrix products, transpose_product(): lax.dot_general(grads, piece, (((1,), (1,)), ((), ())), preferred_element...  9.05 us
    another operation x1, local copies, waits for them, and re-layouts, order_node_up(): jnp.stack([block_here] * axis_size('fsdp'), axis=0)  7.2 us
  transfers between devices with their start and end apart: 2, of which 2 were waited for; matrix products, arithmetic and copies ran while one was open for 8% of the time, Pallas kernels for 0%

profile of v1, /device:TPU:0, one launch (start us, length us, event | category | flops | bytes accessed | tf_op | source)
XLA Modules:
  0.0 283.8 jit_solution(3455203910167941436)
XLA Ops:
  7.2 0.0 copy-start
  7.2 0.0 reduce-scatter.2.cloned.1.call-start
  7.2 2.2 fusion
  9.5 0.2 copy-done
  9.7 11.6 %convolution_convert_fusion = bf16[2048,3072]{1,0:T(8,128)(2,1)} fusion(bf16[1,512,3072]{2,1,0:T(8,128)(2,1)S(1)} %copy-done, bf16[1,512,2048]{2,1,0:T(8,128)(2,1)} %param.10, f32[2048]{0:T(1024)} %bitcast.37, f32[512]{0:T(512)S(1)} %add_rsqrt_fusion), kind=kOutput, calls=%fused_computation | convolution fusion | flops 6452936704 | bytes 17836032 | tf_op jit(solution)/shard_map/dot_general | solution.py:53
  21.3 0.0 reduce-scatter.2.cloned.1.call-update
  21.3 7.2 %stack.3 = bf16[16,128,3072]{2,1,0:T(8,128)(2,1)} broadcast(bf16[128,3072]{1,0:T(8,128)(2,1)} %bitcast.35), dimensions={1,2} | broadcast | bytes 13369344 | tf_op jit(solution)/shard_map/stack | solution.py:39
  28.5 0.0 copy-start.1
  28.5 184.2 %all_to_all.5 = bf16[16,128,3072]{2,1,0:T(8,128)(2,1)S(1)} all-to-all(bf16[16,128,3072]{2,1,0:T(8,128)(2,1)} %stack.3), channel_id=1, replica_groups=mesh['section'=8,'fsdp'=16] {'fsdp'}, dimensions={0} | all-to-all | bytes 25165824 | tf_op jit(solution)/shard_map/all_to_all | solution.py:39
  212.7 0.0 copy-done.1
  212.7 9.1 %fusion.3 = (f32[512]{0:T(512)S(1)}, f32[512]{0:T(512)S(1)}, f32[512,2048]{1,0:T(8,128)S(1)}) fusion(bf16[1,512,2048]{2,1,0:T(8,128)(2,1)} %param.7, f32[2048]{0:T(1024)S(1)} %bitcast.38, bf16[2048,3072]{1,0:T(8,128)(2,1)S(1)} %bitcast.34, bf16[1,512,3072]{2,1,0:T(8,128)(2,1)} %param.9), kind=kOutput, calls=%fused_computation.9 | convolution fusion | flops 6448741376 | bytes 22032384 | tf_op jit(solution)/shard_map/dot_general | solution.py:22
  221.8 5.4 %fusion.8 = bf16[512,2048]{1,0:T(8,128)(2,1)} fusion(f32[512,2048]{1,0:T(8,128)S(1)} %get-tuple-element.5, bf16[1,512,2048]{2,1,0:T(8,128)(2,1)} %param.8, bf16[1,512,2048]{2,1,0:T(8,128)(2,1)} %param.7, f32[512]{0:T(512)S(1)} %get-tuple-element.7, f32[2048]{0:T(1024)S(1)} %bitcast.39, f32[512]{0:T(512)S(1)} %get-tuple-element.6), kind=kLoop, calls=%fused_computation.14 | loop fusion | flops 11534336 | bytes 10498048 | tf_op jit(solution)/shard_map/convert_element_type | solution.py:50
  227.2 1.3 collective-permute-start
  228.5 5.1 %collective-permute-done = bf16[512,2048]{1,0:T(8,128)(2,1)} collective-permute-done((bf16[512,2048]{1,0:T(8,128)(2,1)}, bf16[512,2048]{1,0:T(8,128)(2,1)}, u32[]{:S(2)}, u32[]{:S(2)}) %collective-permute-start) | collective-permute-done | bytes 2097184 | tf_op jit(solution)/shard_map/ppermute | solution.py:13
  233.6 16.1 %reduce-scatter.2.cloned.1.call-done = bf16[128,3072]{1,0:T(8,128)(2,1)} async-done(((bf16[2048,3072]{1,0:T(8,128)(2,1)}), bf16[128,3072]{1,0:T(8,128)(2,1)}) %reduce-scatter.2.cloned.1.call-update) | async-done | bytes 786448 | tf_op jit(solution)/shard_map/reduce_scatter | solution.py:52
  249.7 1.7 fusion.17
  251.4 19.4 %all-gather = f32[16,1,128]{2,1,0:T(1,128)S(1)} all-gather(f32[1,1,128]{2,1,0:T(1,128)S(1)} %fusion.18), channel_id=1, replica_groups=mesh['section'=8,'fsdp'=16] {'fsdp'}, dimensions={0}, use_global_device_ids=true | all-gather | bytes 8704 | tf_op jit(solution)/shard_map/all_gather | solution.py:62
  270.8 2.4 convert_bitcast_fusion
  273.2 3.2 %copy.12 = bf16[1,512,2048]{2,1,0:T(8,128)(2,1)} copy(bf16[1,512,2048]{2,1,0:T(8,128)(2,1)} %bitcast.7) | data formatting | bytes 4194304
  276.4 0.6 copy.13
  (3 shorter events, 0.0 us)
Async XLA Ops:
  7.2 2.5 copy-start
  7.2 242.6 %reduce-scatter.2.cloned.1.call-start = ((), (), s32[]{:S(2)}) async-start(), calls=%async_computation.2 | async-start | bytes 13369344 | tf_op jit(solution)/shard_map/reduce_scatter | solution.py:52
  28.5 184.2 %copy-start.1 = (f32[1,2048]{1,0:T(1,128)S(1)}, f32[1,2048]{1,0:T(1,128)}, u32[]{:S(2)}) copy-start(f32[1,2048]{1,0:T(1,128)} %param.13) | copy-start | bytes 24580
  227.2 6.4 %collective-permute-start = (bf16[512,2048]{1,0:T(8,128)(2,1)}, bf16[512,2048]{1,0:T(8,128)(2,1)}, u32[]{:S(2)}, u32[]{:S(2)}) collective-permute-start(bf16[512,2048]{1,0:T(8,128)(2,1)} %fusion.8), channel_id=1, source_target_pairs={{16,0},{32,16},{48,32},{64,48},{80,64},{96,80},{112,96},{17,1},{33... | collective-permute-start | bytes 6291464 | tf_op jit(solution)/shard_map/ppermute | solution.py:13
Sparse Core Ops, SparseCore 0:
  21.4 228.2 reduce-scatter.1
